TPU v7x, 32 devices: a whole 2x2x4 slice. The times are simulated.
32 devices in a mesh: ctx: 8 (over z, y), tp: 4 (over x, core).
Axes of the slice: x: 2, y: 2, z: 4, core: 2. Of those that a mesh axis runs over, the one named last changes fastest.
Arguments:
- projections: bfloat16 [3, 2048, 4096], P(None, 'ctx', 'tp'), may hold values from -6 to 6
- short_weights: float32 [3, 7, 4096], P(None, None, 'tp'), may hold values from -2 to 2
- skip_gain: float32 [4096], P('tp'), may hold values from -1 to 1
- filters: bfloat16 [256, 128], P('tp'), may hold values from -0.5 to 0.5
- out_weight: bfloat16 [4096, 4096], P('tp'), may hold values from -0.09375 to 0.09375
- out_cotangent: bfloat16 [2048, 4096], P(('ctx', 'tp')), may hold values from -6 to 6
Outputs:
- mixed: bfloat16 [2048, 4096], P(('ctx', 'tp'))
- proj_grad: float32 [3, 2048, 4096], P(None, 'ctx', 'tp')
- filter_grad: float32 [256, 128], P('tp', 'ctx')
All inputs are finite; a program needn't handle non-finite values.
Results may differ from a plain program's by a relative error of at most 0.009.
Values may be sent and summed in bfloat16 or wider, within the bound.
No kernel may reach another device: no remote copies, remote signals or barrier semaphores. Data moves between devices by JAX's collectives and lax.ppermute only.
A program may use at most 128 MiB of HBM per device.

v0:
```python
import math

import jax
import jax.numpy as jnp
from jax import lax
from jax.experimental import pallas as pl
from jax.experimental.pallas import tpu as pltpu
from jax.sharding import PartitionSpec as P

LANES = 128
SIDE = 256
EDGE = 8
COVER = 10**11
BF = jnp.bfloat16
F32 = jnp.float32
NT = (((1,), (1,)), ((), ()))
TN = (((0,), (0,)), ((), ()))


def called(kernel, name, operands, results, scratch=(), kept=(), cover=1, mib=16):
    spaces = [
        pltpu.HBM if position in kept else pltpu.VMEM
        for position in range(len(operands) + len(results))
    ]
    first = len(operands)
    placed = [
        pltpu.with_memory_space_constraint(value, space) for value, space in zip(operands, spaces)
    ]
    return pl.pallas_call(
        kernel,
        name=name,
        in_specs=[pl.BlockSpec(memory_space=space) for space in spaces[:first]],
        out_specs=[pl.BlockSpec(memory_space=space) for space in spaces[first:]],
        out_shape=[space(*result) for space, result in zip(spaces[first:], results)],
        scratch_shapes=list(scratch),
        compiler_params=pltpu.CompilerParams(vmem_limit_bytes=mib << 20),
        cost_estimate=pl.CostEstimate(flops=cover, transcendentals=0, bytes_accessed=1),
    )(*placed)


def repeated(count, body):
    def step(index, carry):
        body(index)
        return carry

    lax.fori_loop(0, count, step, 0)


def unrolled(count, body):
    for index in range(count):
        body(index)


def multiple(value, of):
    return value if isinstance(value, int) else pl.multiple_of(value, of)


def lanes_of(block, half):
    return pl.ds(multiple(block * SIDE + half * LANES, LANES), LANES)


def rows_of(block, size):
    return pl.ds(multiple(block * size, size), size)


def exchanged(value, axis, bit):
    count = lax.axis_size(axis)
    return lax.ppermute(value, axis, [(index, index ^ bit) for index in range(count)])


def passed_along(value, axis, steps):
    count = lax.axis_size(axis)
    initial, last = (max(0, -steps), min(count, count - steps))
    return lax.ppermute(value, axis, [(source, source + steps) for source in range(initial, last)])


def iota(shape, dim):
    return lax.broadcasted_iota(jnp.int32, shape, dim)


def flip_matrix(taps, total, dtype):
    rows, cols = iota((taps, taps), 0), iota((taps, taps), 1)
    return ((rows + cols) % taps == total).astype(F32).astype(dtype)


def skewed(row, height):
    wide = jnp.broadcast_to(row, (height, row.shape[1]))
    return pltpu.roll(wide, 0, 1, stride=1, stride_axis=0)


def group_of_lane(shape, width):
    return (iota(shape, 1) % LANES) // width


def picked(stacked, rows, per, width):
    owner = group_of_lane((rows, stacked.shape[1]), width)
    total = stacked[:rows]
    for member in range(1, per):
        total = jnp.where(owner == member, stacked[member * rows : (member + 1) * rows], total)
    return total


def side_by_side(ext, blocks):
    return jnp.concatenate(
        [ext[block * LANES : (block + 2) * LANES] for block in range(blocks)], axis=1
    )


def short_sum(ref, base, step, weights, rows):
    total = weights[0:1] * ref[pl.ds(base, rows), :]
    for tap in range(1, weights.shape[0]):
        total = total + weights[tap : tap + 1] * ref[pl.ds(base + step * tap, rows), :]
    return total


def tail_kernel(proj_hbm, sw_hbm, out_ref, proj_ref, sw_ref, xs_ref, sems):
    rows, channels = proj_hbm.shape[1:]
    taps = out_ref.shape[0] - 4 * EDGE
    reach = taps + 16
    copies = [
        pltpu.make_async_copy(sw_hbm, sw_ref, sems.at[0]),
        pltpu.make_async_copy(proj_hbm.at[:, pl.ds(rows - reach, reach), :], proj_ref, sems.at[1]),
    ]
    for copy in copies:
        copy.start()
    for copy in copies:
        copy.wait()

    def body(block):
        for half in range(SIDE // LANES):
            lanes = lanes_of(block, half)
            for part in range(1, 3):
                xs_ref[half, part] = proj_ref[part, :, lanes].astype(F32)
            feats = [
                short_sum(xs_ref.at[half, part], 16, -1, sw_ref[part, :, lanes], taps) for part in (1, 2)
            ]
            out_ref[pl.ds(0, taps), lanes] = (feats[0] * feats[1]).astype(BF)
            ends = [proj_ref[part, pl.ds(taps, 16), lanes].astype(F32)[16 - EDGE :] for part in range(3)]
            out_ref[pl.ds(taps, 4 * EDGE), lanes] = jnp.concatenate(
                ends + [jnp.zeros((EDGE, LANES), F32)], axis=0
            ).astype(BF)

    unrolled(channels // SIDE, body)


def gated_tail(projections, short_weights, taps):
    _, rows, channels = projections.shape
    return called(
        tail_kernel, "gated_tail", (projections, short_weights),
        [((taps + 4 * EDGE, channels), BF)],
        scratch=[
            pltpu.VMEM((3, taps + 16, channels), BF),
            pltpu.VMEM(short_weights.shape, F32),
            pltpu.VMEM((2, 3, taps + 16, LANES), F32),
            pltpu.SemaphoreType.DMA((2,)),
        ],
        kept=(0, 1),
    )[0]


def prepare_kernel(
    proj_hbm, sw_hbm, filt_hbm, w_hbm, skip_hbm, after_hbm,
    feat_ref, edge_ref, gated_ref, fwd_ref, bwd_ref, sw_ref, skip_ref, w_ref,
    proj_ref, filt_ref, xs_ref, sems,
):
    rows, channels = proj_ref.shape[1:]
    groups, taps = filt_ref.shape
    per = groups * SIDE // channels
    copies = [
        pltpu.make_async_copy(source, target, sems.at[index])
        for index, (source, target) in enumerate(
            (
                (filt_hbm, filt_ref), (proj_hbm, proj_ref), (sw_hbm, sw_ref), (skip_hbm, skip_ref),
                (w_hbm, w_ref),
            )
        )
    ]
    for copy in copies:
        copy.start()
    shape = (taps, taps)
    inside = iota(shape, 1) <= iota(shape, 0)
    later = iota(shape, 1) >= iota(shape, 0)
    copies[0].wait()

    def build(block):
        plain = filt_ref[rows_of(block, per), :]
        turned = jnp.dot(plain, flip_matrix(taps, 0, BF), preferred_element_type=F32)
        plain = plain.astype(F32)
        for member in range(per):
            place = pl.ds(multiple((block * per + member) * taps, taps), taps)
            turn = skewed(turned[member : member + 1], taps)
            fwd_ref[place, pl.ds(0, taps)] = jnp.where(inside, 0.0, turn).astype(BF)
            fwd_ref[place, pl.ds(taps, taps)] = jnp.where(inside, turn, 0.0).astype(BF)
            turn = skewed(plain[member : member + 1], taps)
            bwd_ref[place, pl.ds(0, taps)] = jnp.where(later, turn, 0.0).astype(BF)
            bwd_ref[place, pl.ds(taps, taps)] = jnp.where(later, 0.0, turn).astype(BF)

    repeated(channels // SIDE, build)
    for copy in copies[1:4]:
        copy.wait()

    def features(block):
        for half in range(SIDE // LANES):
            lanes = lanes_of(block, half)
            feats = []
            for part in range(3):
                xs = xs_ref.at[half, part]
                xs[pl.ds(0, EDGE), :] = jnp.zeros((EDGE, LANES), F32)
                full = proj_ref[part, :, lanes].astype(F32)
                xs[pl.ds(EDGE, rows), :] = full
                edge_ref[part, :, lanes] = full[:EDGE]
                feats.append(short_sum(xs, EDGE, -1, sw_ref[part, :, lanes], rows))
                feat_ref[part, :, lanes] = feats[part]
            gated_ref[:, lanes] = (feats[1] * feats[2]).astype(BF)

    repeated(channels // SIDE, features)
    copies[4].wait()


def prepare(projections, short_weights, filters, out_weight, skip, after):
    _, rows, channels = projections.shape
    groups, taps = filters.shape
    return called(
        prepare_kernel, "prepare", (projections, short_weights, filters, out_weight, skip, after),
        [
            ((3, rows, channels), F32),
            ((3, EDGE, channels), F32),
            ((rows, channels), BF),
            ((groups * taps, 2 * taps), BF),
            ((groups * taps, 2 * taps), BF),
            (short_weights.shape, F32),
            (skip.shape, F32),
            (out_weight.shape, BF),
        ],
        scratch=[
            pltpu.VMEM(projections.shape, BF),
            pltpu.VMEM(filters.shape, BF),
            pltpu.VMEM((2, 3, rows + EDGE, LANES), F32),
            pltpu.SemaphoreType.DMA((5,)),
        ],
        kept=(0, 1, 2, 3, 4),
        cover=COVER,
    )


def block_conv(table, ext, taps, per, width):
    blocks = ext.shape[0] // taps - 1
    stacked = jnp.dot(table, side_by_side(ext, blocks), preferred_element_type=F32)
    conv = picked(stacked, taps, per, width)
    return jnp.concatenate(
        [conv[:, block * LANES : (block + 1) * LANES] for block in range(blocks)], axis=0
    )


def halving_order(count):
    order = [0]
    for bit in reversed(bits_of(count)):
        order = order + [index | bit for index in order]
    return order


def forward_kernel(
    feat_ref, edge_ref, gated_ref, halo_ref, sw_ref, skip_ref, table_ref,
    first_ref, long_ref, gext_ref, mix_ref, xs_ref,
):
    rows, channels = gated_ref.shape
    taps = table_ref.shape[1] // 2
    per = table_ref.shape[0] // taps * LANES // channels
    width = LANES // per

    def body(block):
        for half in range(SIDE // LANES):
            lanes = lanes_of(block, half)
            ends = halo_ref[pl.ds(taps, 4 * EDGE), lanes].astype(F32)
            firsts = []
            for part in range(3):
                xs = xs_ref.at[half, part]
                xs[pl.ds(0, EDGE), :] = ends[part * EDGE : (part + 1) * EDGE]
                xs[pl.ds(EDGE, EDGE), :] = edge_ref[part, :, lanes]
                firsts.append(short_sum(xs, EDGE, -1, sw_ref[part, :, lanes], EDGE))
                first_ref[part, :, lanes] = firsts[part]
            begun = jnp.concatenate(
                [firsts[1] * firsts[2], gated_ref[pl.ds(0, 16), lanes].astype(F32)[EDGE:]], axis=0
            ).astype(BF)
            gext_ref[pl.ds(0, taps), lanes] = halo_ref[pl.ds(0, taps), lanes]
            gext_ref[pl.ds(taps, 16), lanes] = begun
            gext_ref[pl.ds(taps + 16, rows - 16), lanes] = gated_ref[pl.ds(16, rows - 16), lanes]
            ext = gext_ref[:, lanes]
            table = table_ref[rows_of(block * 2 + half, per * taps), :]
            long_out = block_conv(table, ext, taps, per, width) + skip_ref[:, lanes] * ext[taps:].astype(F32)
            long_ref[:, lanes] = long_out
            query = jnp.concatenate([firsts[0], feat_ref[0, pl.ds(EDGE, rows - EDGE), lanes]], axis=0)
            mix_ref[:, lanes] = (query * long_out).astype(BF)

    unrolled(channels // SIDE, body)


def forward(feats, edges, gated, halo, short_weights, skip, table):
    _, rows, channels = feats.shape
    taps = table.shape[1] // 2
    return called(
        forward_kernel, "forward", (feats, edges, gated, halo, short_weights, skip, table),
        [
            ((3, EDGE, channels), F32),
            ((rows, channels), F32),
            ((rows + taps, channels), BF),
            ((rows, channels), BF),
        ],
        scratch=[pltpu.VMEM((2, 3, 2 * EDGE, LANES), F32)],
        cover=COVER,
    )


def project_kernel(own, mix_ref, w_ref, *refs):
    term_refs = refs[-2:]
    rows = mix_ref.shape[0]
    me = lax.axis_index("tp")
    order = halving_order(rows // own)
    ordered = jnp.concatenate([mix_ref[rows_of(me ^ k, own), :] for k in order], axis=0)
    kept = term_refs[0].shape[0]
    chunk = 512

    def project(block):
        cols = pl.ds(multiple(block * chunk, chunk), chunk)
        terms = jnp.dot(ordered, w_ref[:, cols], preferred_element_type=F32).astype(BF)
        term_refs[0][:, cols] = terms[:kept]
        if kept < rows:
            term_refs[1][:, cols] = terms[kept:]

    repeated(w_ref.shape[1] // chunk, project)


def project(mixer_out, out_weight, after, n_tp):
    rows, features = mixer_out.shape[0], out_weight.shape[1]
    own = rows // n_tp
    split = [rows // 2] * 2 if n_tp > 1 else [rows]
    return called(
        lambda *refs: project_kernel(own, *refs), "project", (mixer_out, out_weight, *after),
        [((size, features), BF) for size in split],
    )


def grads_kernel(n_tp, *refs):
    pieces, (w_ref, grad_ref, cot_ref) = refs[:n_tp], refs[n_tp:]
    rows, channels = grad_ref.shape
    own = rows // n_tp
    me = lax.axis_index("tp")
    for k in range(n_tp):
        cot_ref[rows_of(me ^ k, own), :] = pieces[k][...]

    def body(block):
        place = rows_of(block, SIDE)
        grad_ref[:, place] = lax.dot_general(
            cot_ref[...], w_ref[place, :], NT, preferred_element_type=F32
        )

    unrolled(channels // SIDE, body)


def mixer_grads(pieces, out_weight):
    n_tp = len(pieces)
    channels, features = out_weight.shape
    rows = pieces[0].shape[0] * n_tp
    return called(
        lambda *refs: grads_kernel(n_tp, *refs), "grads", (*pieces, out_weight),
        [((rows, channels), F32)],
        scratch=[pltpu.VMEM((rows, features), BF)],
    )[0]


def backward_kernel(
    grad_ref, feat_ref, first_ref, long_ref, skip_ref, table_ref, lgrad_ref, qgrad_ref, head_ref
):
    rows, channels = lgrad_ref.shape
    taps = table_ref.shape[1] // 2
    groups = table_ref.shape[0] // taps
    per = groups * LANES // channels
    width = LANES // per

    def body(block):
        for half in range(SIDE // LANES):
            lanes = lanes_of(block, half)
            grad = grad_ref[:, lanes]
            query = grad * long_ref[:, lanes]
            qgrad_ref[:, lanes] = query
            feat = jnp.concatenate(
                [first_ref[0, :, lanes], feat_ref[0, pl.ds(EDGE, rows - EDGE), lanes]], axis=0
            )
            lgrad = (grad * feat).astype(BF)
            lgrad_ref[:, lanes] = lgrad
            first = multiple((block * 2 + half) * per * taps, taps)
            top = jnp.concatenate(
                [table_ref[pl.ds(first + member * taps, 16), :] for member in range(per)], axis=0
            )
            stacked = jnp.dot(top, lgrad[: 2 * taps], preferred_element_type=F32)
            gated_grad = picked(stacked, 16, per, width) + skip_ref[:, lanes] * lgrad[:16].astype(F32)
            head_ref[pl.ds(0, taps), lanes] = lgrad[:taps]
            head_ref[pl.ds(taps, 4 * EDGE), lanes] = jnp.concatenate(
                [
                    query[:EDGE],
                    gated_grad[:EDGE] * first_ref[2, :, lanes],
                    gated_grad[:EDGE] * first_ref[1, :, lanes],
                    jnp.zeros((EDGE, LANES), F32),
                ],
                axis=0,
            ).astype(BF)

    unrolled(channels // SIDE, body)


def backward(grads, feats, firsts, long_out, skip, table):
    rows, channels = long_out.shape
    taps = table.shape[1] // 2
    return called(
        backward_kernel, "backward", (grads, feats, firsts, long_out, skip, table),
        [((rows, channels), BF), ((rows, channels), F32), ((taps + 4 * EDGE, channels), BF)],
    )


def lag_kernel(count, lgrad_ref, gext_ref, after_ref, lag_ref, lags_ref, turn_ref):
    rows, channels = lgrad_ref.shape
    groups, taps = lags_ref.shape
    per = groups * LANES // channels
    width = LANES // per
    blocks = rows // taps
    square = (taps, taps)
    inside = iota(square, 1) + iota(square, 0) < taps
    reverse = flip_matrix(taps, taps - 1, BF)

    def body(block):
        sums = []
        for half in range(SIDE // LANES):
            lanes = lanes_of(block, half)
            wide = jnp.concatenate(
                [lgrad_ref[pl.ds(part * taps, taps), lanes] for part in range(blocks)], axis=1
            )
            wide = jnp.dot(reverse, wide, preferred_element_type=F32).astype(BF)
            owner = group_of_lane((1, wide.shape[1]), width)
            left = jnp.concatenate(
                [wide * (owner == member).astype(F32).astype(BF) for member in range(per)], axis=0
            )
            scores = lax.dot_general(
                left, side_by_side(gext_ref[:, lanes], blocks), NT, preferred_element_type=F32
            )
            for member in range(per):
                score = scores[member * taps : (member + 1) * taps]
                merged = jnp.where(inside, score[:, taps:], score[:, :taps])
                merged = pltpu.roll(merged, 0, 1, stride=1, stride_axis=0)
                sums.append(jnp.sum(merged, axis=0, keepdims=True))
        lags_ref[rows_of(block, len(sums)), :] = jnp.concatenate(sums, axis=0)

    unrolled(channels // SIDE, body)
    turn_ref[...] = lax.dot_general(
        flip_matrix(taps, taps - 1, F32), lags_ref[...], NT,
        precision=lax.Precision.HIGHEST, preferred_element_type=F32,
    )
    if count == 1:
        lag_ref[...] = turn_ref[...]
        return
    here, share = lax.axis_index("ctx"), taps // count
    for k in range(count):
        lag_ref[pl.ds(k * share, share), :] = turn_ref[rows_of(here ^ k, share), :]


def lag_sums(lgrad, gext, groups, count, after):
    rows, channels = lgrad.shape
    taps = gext.shape[0] - rows
    return called(
        lambda *refs: lag_kernel(count, *refs), "lag_sums", (lgrad, gext, after),
        [((taps, groups), F32)],
        scratch=[pltpu.VMEM((groups, taps), F32), pltpu.VMEM((taps, groups), F32)],
    )[0]


def feature_kernel(lgrad_ref, head_ref, qgrad_ref, feat_ref, first_ref, skip_ref, table_ref, fg_ref):
    rows, channels = lgrad_ref.shape
    taps = table_ref.shape[1] // 2
    per = table_ref.shape[0] // taps * LANES // channels
    width = LANES // per
    rest = pl.ds(EDGE, rows - EDGE)

    def body(block):
        for half in range(SIDE // LANES):
            lanes = lanes_of(block, half)
            lgrad = lgrad_ref[:, lanes]
            ext = jnp.concatenate([lgrad, head_ref[pl.ds(0, taps), lanes]], axis=0)
            table = table_ref[rows_of(block * 2 + half, per * taps), :]
            gated_grad = block_conv(table, ext, taps, per, width) + skip_ref[:, lanes] * lgrad.astype(F32)
            heads = head_ref[pl.ds(taps, 4 * EDGE), lanes].astype(F32)
            for part in range(3):
                fg = fg_ref.at[block * 2 + half, part]
                if part:
                    fg[pl.ds(0, EDGE), :] = gated_grad[:EDGE] * first_ref[3 - part, :, lanes]
                    fg[rest, :] = gated_grad[EDGE:] * feat_ref[3 - part, rest, lanes]
                else:
                    fg[pl.ds(0, rows), :] = qgrad_ref[:, lanes]
                fg[pl.ds(rows, EDGE), :] = heads[part * EDGE : (part + 1) * EDGE]

    unrolled(channels // SIDE, body)


def feature_grads(lgrad, heads, qgrad, feats, firsts, skip, table):
    rows, channels = lgrad.shape
    return called(
        feature_kernel, "feature_grads", (lgrad, heads, qgrad, feats, firsts, skip, table),
        [((channels // LANES, 3, rows + EDGE, LANES), F32)],
    )[0]


def short_grads_kernel(fg_ref, sw_ref, out_ref, res_ref, sems):
    rows, channels = out_ref.shape[1:]

    def copy_of(block):
        lanes = pl.ds(multiple(block * SIDE, SIDE), SIDE)
        return pltpu.make_async_copy(res_ref.at[:, :, lanes], out_ref.at[:, :, lanes], sems.at[block])

    def body(block):
        for half in range(SIDE // LANES):
            lanes = lanes_of(block, half)
            for part in range(3):
                fg = fg_ref.at[block * 2 + half, part]
                res_ref[part, :, lanes] = short_sum(fg, 0, 1, sw_ref[part, :, lanes], rows)
        copy_of(block).start()

    unrolled(channels // SIDE, body)
    for block in range(channels // SIDE):
        copy_of(block).wait()


def short_grads(fgs, short_weights):
    blocks, _, rows, _ = fgs.shape
    rows, channels = rows - EDGE, blocks * LANES
    return called(
        short_grads_kernel, "short_grads", (fgs, short_weights),
        [((3, rows, channels), F32)],
        scratch=[
            pltpu.VMEM((3, rows, channels), F32),
            pltpu.SemaphoreType.DMA((channels // SIDE,)),
        ],
        kept=(2,),
    )[0]


def last_kernel(factor, term_ref, final_ref, lag_ref, arrived_ref, mixed_hbm, filter_hbm, mixed_ref, filter_ref, sems):
    own = mixed_ref.shape[0]
    mixed = term_ref[pl.ds(0, own), :].astype(F32)
    if final_ref.shape[0] == own:
        mixed = mixed + final_ref[...].astype(F32)
    mixed_ref[...] = mixed.astype(BF)
    total = lag_ref[pl.ds(0, filter_ref.shape[0]), :]
    if arrived_ref.shape == filter_ref.shape:
        total = total + arrived_ref[...]
    filter_ref[...] = total * factor
    copies = [
        pltpu.make_async_copy(mixed_ref, mixed_hbm, sems.at[0]),
        pltpu.make_async_copy(filter_ref, filter_hbm, sems.at[1]),
    ]
    for copy in copies:
        copy.start()
    for copy in copies:
        copy.wait()


def last(terms, final, lags, arrived, own, share, factor):
    results = [((own, terms.shape[1]), BF), ((share, lags.shape[1]), F32)]
    return called(
        lambda *refs: last_kernel(factor, *refs), "last", (terms, final, lags, arrived), results,
        scratch=[pltpu.VMEM(*result) for result in results] + [pltpu.SemaphoreType.DMA((2,))],
        kept=(4, 5),
    )


def bits_of(count):
    return [1 << position for position in range(count.bit_length() - 1)]


def shards(projections, short_weights, skip_gain, filters, out_weight, out_cotangent):
    _, rows, channels = projections.shape
    group_count, taps = filters.shape
    n_tp, n_ctx = lax.axis_size("tp"), lax.axis_size("ctx")
    skip = skip_gain.reshape(1, channels)

    pack = gated_tail(projections, short_weights, taps)
    halo = passed_along(pack, "ctx", 1)

    feats, edges, gated, fwd_table, bwd_table, weights, skip, out_weight = prepare(
        projections, short_weights, filters, out_weight, skip, pack
    )
    pieces = {0: out_cotangent}
    for bit in reversed(bits_of(n_tp)):
        pieces.update({k | bit: exchanged(piece, "tp", bit) for k, piece in list(pieces.items())})
    pieces = [pieces[k] for k in range(n_tp)]

    firsts, long_out, gext, mixer_out = forward(feats, edges, gated, halo, weights, skip, fwd_table)
    terms = project(mixer_out, out_weight, pieces[1::2], n_tp)
    grads = mixer_grads(pieces, out_weight)
    lgrad, qgrad, heads = backward(grads, feats, firsts, long_out, skip, bwd_table)
    later = passed_along(heads, "ctx", -1)

    own = rows // n_tp
    held = after = final = terms[0]
    sent = terms[-1]
    for bit in bits_of(n_tp):
        arrived = exchanged(sent, "tp", bit)
        if bit == 1:
            arrived, lgrad = lax.optimization_barrier((arrived, lgrad))
        if 2 * bit == n_tp:
            final = arrived
            break
        held = held.astype(F32) + arrived.astype(F32)
        half = held.shape[0] // 2
        sent = after = held[half:].astype(BF)
        held = held[:half]

    share = taps // n_ctx
    apart = share % EDGE == 0
    lags = lag_sums(lgrad, gext, group_count, n_ctx if apart else 1, after)
    fgs = feature_grads(lgrad, later, qgrad, feats, firsts, skip, bwd_table)
    proj_grad = short_grads(fgs, weights)
    arrived = lags
    for position, bit in enumerate(reversed(bits_of(n_ctx)) if apart else ()):
        if position:
            lags = lags[: bit * share * 2] + arrived
        arrived = exchanged(lags[bit * share :], "ctx", bit)
        if position == 0:
            arrived, later = lax.optimization_barrier((arrived, later))
        if position == 1:
            arrived, final = lax.optimization_barrier((arrived, final))
    if not apart:
        lags = arrived = lax.psum_scatter(lags, "ctx", scatter_dimension=0, tiled=True)
    factor = 1.0 / math.sqrt(rows * n_ctx * (channels // group_count))
    if not apart:
        arrived = final
    mixed, filter_grad = last(held, final, lags, arrived, own, share, factor)
    filter_grad = filter_grad.T
    return (mixed, proj_grad, filter_grad)


def solution(mesh):
    placed = (
        P(None, "ctx", "tp"),
        P(None, None, "tp"),
        P("tp"),
        P("tp", None),
        P("tp", None),
        P(("ctx", "tp"), None),
    )
    return jax.shard_map(
        shards,
        mesh=mesh,
        in_specs=placed,
        out_specs=(P(("ctx", "tp"), None), P(None, "ctx", "tp"), P("tp", "ctx")),
        check_vma=False,
    )
```

profile of v0, /device:TPU:0, one launch (start us, length us, event | category | flops | bytes accessed | tf_op | source)
XLA Modules:
  0.0 51.4 jit_solution(5130047594377667265)
XLA Ops:
  0.6 3.0 %collective-permute-start.2 = (bf16[64,4096]{1,0:T(8,128)(2,1)}, bf16[64,4096]{1,0:T(8,128)(2,1)S(1)}, u32[]{:S(2)}, u32[]{:S(2)}) collective-permute-start(bf16[64,4096]{1,0:T(8,128)(2,1)} %refs_0_.1), channel_id=1, source_target_pairs={{0,2},{1,3},{2,0},{3,1},{4,6},{5,7},{6,4},{7,5},{8,10},{9,11},{10,... | collective-permute-start | bytes 1572872 | tf_op jit(solution)/shard_map/ppermute | solution.py:68
  3.6 0.0 collective-permute-start.1
  3.6 1.9 %gated_tail.1.after_hbm = bf16[160,1024]{1,0:T(8,128)(2,1)S(1)} custom-call(bf16[3,256,1024]{2,1,0:T(8,128)(2,1)} %proj_hbm.3, f32[3,7,1024]{2,1,0:T(8,128)} %sw_hbm.3), custom_call_target="tpu_custom_call" | custom-call | flops 1 | bytes 1 | tf_op jit(solution)/shard_map/gated_tail/pallas_call | solution.py:29
  5.5 3.4 %collective-permute-start = (bf16[160,1024]{1,0:T(8,128)(2,1)S(1)}, bf16[160,1024]{1,0:T(8,128)(2,1)S(1)}, u32[]{:S(2)}, u32[]{:S(2)}) collective-permute-start(bf16[160,1024]{1,0:T(8,128)(2,1)S(1)} %gated_tail.1.after_hbm), channel_id=1, source_target_pairs={{0,4},{4,8},{8,12},{12,16},{16,20},{20,24},{24,28},{1,5},{5,9},{9,... | collective-permute-start | bytes 983048 | tf_op jit(solution)/shard_map/ppermute | solution.py:74
  8.9 5.6 %prepare.1 = (f32[3,256,1024]{2,1,0:T(8,128)S(1)}, f32[3,8,1024]{2,1,0:T(8,128)S(1)}, bf16[256,1024]{1,0:T(8,128)(2,1)S(1)}, bf16[8192,256]{1,0:T(8,128)(2,1)S(1...) custom-call(bf16[3,256,1024]{2,1,0:T(8,128)(2,1)} %proj_hbm.3, ...), custom_call_target="tpu_custom_call" | custom-call | flops 99999997952 | bytes 1 | tf_op jit(solution)/shard_map/prepare/pallas_call | solution.py:29
  14.6 1.2 %collective-permute-done.2.refs_2_ = bf16[64,4096]{1,0:T(8,128)(2,1)S(1)} collective-permute-done((bf16[64,4096]{1,0:T(8,128)(2,1)}, bf16[64,4096]{1,0:T(8,128)(2,1)S(1)}, u32[]{:S(2)}, u32[]{:S(2)}) %collective-permute-start.2) | collective-permute-done | bytes 524320 | tf_op jit(solution)/shard_map/ppermute | solution.py:68
  15.8 0.0 collective-permute-start.3
  15.8 0.8 %collective-permute-done.halo_ref = bf16[160,1024]{1,0:T(8,128)(2,1)S(1)} collective-permute-done((bf16[160,1024]{1,0:T(8,128)(2,1)S(1)}, bf16[160,1024]{1,0:T(8,128)(2,1)S(1)}, u32[]{:S(2)}, u32[]{:S(2)}) %collective-permute-start) | collective-permute-done | bytes 327712 | tf_op jit(solution)/shard_map/ppermute | solution.py:74
  16.6 1.5 %forward.1 = (f32[3,8,1024]{2,1,0:T(8,128)S(1)}, f32[256,1024]{1,0:T(8,128)S(1)}, bf16[384,1024]{1,0:T(8,128)(2,1)S(1)}, bf16[256,1024]{1,0:T(8,128)(2,1)S(1)}) custom-call(f32[3,256,1024]{2,1,0:T(8,128)S(1)} %get-tuple-element.27.feat_ref, f32[3,8,1024]{2,1,0:T(8,128)S(1)} %get-tuple-element.28.edge_ref, bf16[256,1024]{1,0:T(8,128)(2,1)S(1)} %get-tuple-element.29.gated_ref, ...), custom_call_target="tpu_custom_call" | custom-call | flops 99999997952 | bytes 1 | tf_op jit(solution)/shard_map/forward/pallas_call | solution.py:29
  18.1 0.0 collective-permute-done.1.refs_2_.refs_1_
  18.1 0.0 collective-permute-done.3.refs_3_
  18.1 0.0 copy-start
  18.1 4.7 %project.1 = (bf16[128,4096]{1,0:T(8,128)(2,1)S(1)}, bf16[128,4096]{1,0:T(8,128)(2,1)S(1)}) custom-call(bf16[256,1024]{1,0:T(8,128)(2,1)S(1)} %get-tuple-element.33.refs_0_, bf16[1024,4096]{1,0:T(8,128)(2,1)S(1)} %get-tuple-element.34.refs_1_.refs_4_, bf16[64,4096]{1,0:T(8,128)(2,1)} %collective-permute-done.1.refs_2_.refs_1_, ...), custom_call_target="tpu_custom_call" | custom-call | flops 1 | bytes 1 | tf_op jit(solution)/shard_map/project/pallas_call | solution.py:29
  22.8 0.1 collective-permute-start.4
  22.9 0.0 copy-done
  22.9 3.5 %grads.1.grad_ref = f32[256,1024]{1,0:T(8,128)S(1)} custom-call(bf16[64,4096]{1,0:T(8,128)(2,1)S(1)} %copy-done, bf16[64,4096]{1,0:T(8,128)(2,1)} %collective-permute-done.1.refs_2_.refs_1_, bf16[64,4096]{1,0:T(8,128)(2,1)S(1)} %collective-permute-done.2.refs_2_, bf16[64,4096]{1,0:T(8,128)(2,1)S(1)} %collective-permute-done.3.refs_3_, ...), custom_call_target="tpu_custom_call" | custom-call | flops 1 | bytes 1 | tf_op jit(solution)/shard_map/grads/pallas_call | solution.py:29
  26.4 0.5 backward.1
  26.9 1.3 %collective-permute-start.6 = (bf16[160,1024]{1,0:T(8,128)(2,1)S(1)}, bf16[160,1024]{1,0:T(8,128)(2,1)S(1)}, u32[]{:S(2)}, u32[]{:S(2)}) collective-permute-start(bf16[160,1024]{1,0:T(8,128)(2,1)S(1)} %get-tuple-element.44), channel_id=1, source_target_pairs={{4,0},{8,4},{12,8},{16,12},{20,16},{24,20},{28,24},{5,1},{9,5},{13... | collective-permute-start | bytes 983048 | tf_op jit(solution)/shard_map/ppermute | solution.py:74
  28.2 0.0 collective-permute-done.4
  28.2 0.3 convert_add_fusion
  28.4 0.1 slice.39.refs_2_
  28.5 1.5 %collective-permute-start.8 = (bf16[64,4096]{1,0:T(8,128)(2,1)S(1)}, bf16[64,4096]{1,0:T(8,128)(2,1)S(1)}, u32[]{:S(2)}, u32[]{:S(2)}) collective-permute-start(bf16[64,4096]{1,0:T(8,128)(2,1)S(1)} %slice.39.refs_2_), channel_id=1, source_target_pairs={{0,2},{1,3},{2,0},{3,1},{4,6},{5,7},{6,4},{7,5},{8,10},{9,11},{10,... | collective-permute-start | bytes 1572872 | tf_op jit(solution)/shard_map/ppermute | solution.py:68
  30.0 2.1 %lag_sums.1 = f32[128,64]{1,0:T(8,128)S(1)} custom-call(bf16[256,1024]{1,0:T(8,128)(2,1)S(1)} %get-tuple-element.42.refs_0_.lgrad_ref, bf16[384,1024]{1,0:T(8,128)(2,1)S(1)} %get-tuple-element.43.refs_1_, bf16[64,4096]{1,0:T(8,128)(2,1)S(1)} %slice.39.refs_2_), custom_call_target="tpu_custom_call" | custom-call | flops 1 | bytes 1 | tf_op jit(solution)/shard_map/lag_sums/pallas_call | solution.py:29
  32.1 4.7 %collective-permute-start.5 = (f32[64,64]{1,0:T(8,128)S(1)}, f32[64,64]{1,0:T(8,128)S(1)}, u32[]{:S(2)}, u32[]{:S(2)}) collective-permute-start(f32[64,64]{1,0:T(8,128)S(1)} %slice.32), channel_id=1, source_target_pairs={{0,16},{4,20},{8,24},{12,28},{16,0},{20,4},{24,8},{28,12},{1,17},{... | collective-permute-start | bytes 49160 | tf_op jit(solution)/shard_map/ppermute | solution.py:68
  36.9 2.7 %collective-permute-done.6.head_ref = bf16[160,1024]{1,0:T(8,128)(2,1)S(1)} collective-permute-done((bf16[160,1024]{1,0:T(8,128)(2,1)S(1)}, bf16[160,1024]{1,0:T(8,128)(2,1)S(1)}, u32[]{:S(2)}, u32[]{:S(2)}) %collective-permute-start.6) | collective-permute-done | bytes 327712 | tf_op jit(solution)/shard_map/ppermute | solution.py:74
  39.6 3.0 %collective-permute-done.5 = f32[64,64]{1,0:T(8,128)S(1)} collective-permute-done((f32[64,64]{1,0:T(8,128)S(1)}, f32[64,64]{1,0:T(8,128)S(1)}, u32[]{:S(2)}, u32[]{:S(2)}) %collective-permute-start.5) | collective-permute-done | bytes 16416 | tf_op jit(solution)/shard_map/ppermute | solution.py:68
  42.6 1.5 %collective-permute-start.7 = (f32[32,64]{1,0:T(8,128)S(1)}, f32[32,64]{1,0:T(8,128)S(1)}, u32[]{:S(2)}, u32[]{:S(2)}) collective-permute-start(f32[32,64]{1,0:T(8,128)S(1)} %slice.33), channel_id=1, source_target_pairs={{0,8},{4,12},{8,0},{12,4},{16,24},{20,28},{24,16},{28,20},{1,9},{5... | collective-permute-start | bytes 24584 | tf_op jit(solution)/shard_map/ppermute | solution.py:68
  44.1 2.3 %collective-permute-done.7 = f32[32,64]{1,0:T(8,128)S(1)} collective-permute-done((f32[32,64]{1,0:T(8,128)S(1)}, f32[32,64]{1,0:T(8,128)S(1)}, u32[]{:S(2)}, u32[]{:S(2)}) %collective-permute-start.7) | collective-permute-done | bytes 8224 | tf_op jit(solution)/shard_map/ppermute | solution.py:68
  46.4 0.0 collective-permute-done.8.refs_1_
  46.4 0.1 collective-permute-start.9
  46.5 1.6 %feature_grads.1.fg_ref = f32[8,3,264,128]{3,2,1,0:T(8,128)S(1)} custom-call(bf16[256,1024]{1,0:T(8,128)(2,1)S(1)} %get-tuple-element.42.refs_0_.lgrad_ref, bf16[160,1024]{1,0:T(8,128)(2,1)S(1)} %collective-permute-done.6.head_ref, f32[256,1024]{1,0:T(8,128)S(1)} %get-tuple-element.49.qgrad_ref, f32[3,256,1024]{2,1,0:T(8,128)S(1)} %get-tuple-element.27.feat_ref, ...), custom_call_target="tpu_custom_call" | custom-call | flops 1 | bytes 1 | tf_op jit(solution)/shard_map/feature_grads/pallas_call | solution.py:29
  48.1 2.3 %short_grads.1 = f32[3,256,1024]{2,1,0:T(8,128)} custom-call(f32[8,3,264,128]{3,2,1,0:T(8,128)S(1)} %feature_grads.1.fg_ref, f32[3,7,1024]{2,1,0:T(8,128)S(1)} %get-tuple-element.30.sw_ref), custom_call_target="tpu_custom_call" | custom-call | flops 1 | bytes 1 | tf_op jit(solution)/shard_map/short_grads/pallas_call | solution.py:29
  50.4 0.1 slice.29.refs_0_
  50.5 0.0 collective-permute-done.9.refs_3_
  50.5 0.9 %last.1 = (bf16[64,4096]{1,0:T(8,128)(2,1)}, f32[16,64]{1,0:T(8,128)}) custom-call(f32[64,4096]{1,0:T(8,128)S(1)} %slice.29.refs_0_, bf16[64,4096]{1,0:T(8,128)(2,1)S(1)} %collective-permute-done.8.refs_1_, f32[32,64]{1,0:T(8,128)S(1)} %slice_add_fusion.1.refs_2_, f32[16,64]{1,0:T(8,128)S(1)} %collective-permute-done.9.refs_3_), custom_call_target="tpu_custom_call" | custom-call | flops 1 | bytes 1 | tf_op jit(solution)/shard_map/last/pallas_call | solution.py:29
  (5 shorter events, 0.0 us)
Async XLA Ops:
  0.6 15.1 %collective-permute-start.2 = (bf16[64,4096]{1,0:T(8,128)(2,1)}, bf16[64,4096]{1,0:T(8,128)(2,1)S(1)}, u32[]{:S(2)}, u32[]{:S(2)}) collective-permute-start(bf16[64,4096]{1,0:T(8,128)(2,1)} %refs_0_.1), channel_id=1, source_target_pairs={{0,2},{1,3},{2,0},{3,1},{4,6},{5,7},{6,4},{7,5},{8,10},{9,11},{10,... | collective-permute-start | bytes 1572872 | tf_op jit(solution)/shard_map/ppermute | solution.py:68
  3.6 14.5 %collective-permute-start.1 = (bf16[64,4096]{1,0:T(8,128)(2,1)}, bf16[64,4096]{1,0:T(8,128)(2,1)}, u32[]{:S(2)}, u32[]{:S(2)}) collective-permute-start(bf16[64,4096]{1,0:T(8,128)(2,1)} %refs_0_.1), channel_id=1, source_target_pairs={{0,1},{1,0},{2,3},{3,2},{4,5},{5,4},{6,7},{7,6},{8,9},{9,8},{10,11... | collective-permute-start | bytes 1572872 | tf_op jit(solution)/shard_map/ppermute | solution.py:68
  5.5 11.1 %collective-permute-start = (bf16[160,1024]{1,0:T(8,128)(2,1)S(1)}, bf16[160,1024]{1,0:T(8,128)(2,1)S(1)}, u32[]{:S(2)}, u32[]{:S(2)}) collective-permute-start(bf16[160,1024]{1,0:T(8,128)(2,1)S(1)} %gated_tail.1.after_hbm), channel_id=1, source_target_pairs={{0,4},{4,8},{8,12},{12,16},{16,20},{20,24},{24,28},{1,5},{5,9},{9,... | collective-permute-start | bytes 983048 | tf_op jit(solution)/shard_map/ppermute | solution.py:74
  15.8 2.3 %collective-permute-start.3 = (bf16[64,4096]{1,0:T(8,128)(2,1)S(1)}, bf16[64,4096]{1,0:T(8,128)(2,1)S(1)}, u32[]{:S(2)}, u32[]{:S(2)}) collective-permute-start(bf16[64,4096]{1,0:T(8,128)(2,1)S(1)} %collective-permute-done.2.refs_2_), channel_id=1, source_target_pairs={{0,1},{1,0},{2,3},{3,2},{4,5},{5,4},{6,7},{7,6},{8,9},{9,8},{10,11... | collective-permute-start | bytes 1572872 | tf_op jit(solution)/shard_map/ppermute | solution.py:68
  18.1 4.8 %copy-start = (bf16[64,4096]{1,0:T(8,128)(2,1)S(1)}, bf16[64,4096]{1,0:T(8,128)(2,1)}, u32[]{:S(2)}) copy-start(bf16[64,4096]{1,0:T(8,128)(2,1)} %refs_0_.1) | copy-start | bytes 1572868
  22.8 5.4 %collective-permute-start.4 = (bf16[128,4096]{1,0:T(8,128)(2,1)S(1)}, bf16[128,4096]{1,0:T(8,128)(2,1)S(1)}, u32[]{:S(2)}, u32[]{:S(2)}) collective-permute-start(bf16[128,4096]{1,0:T(8,128)(2,1)S(1)} %get-tuple-element.36), channel_id=1, source_target_pairs={{0,1},{1,0},{2,3},{3,2},{4,5},{5,4},{6,7},{7,6},{8,9},{9,8},{10,11... | collective-permute-start | bytes 3145736 | tf_op jit(solution)/shard_map/ppermute | solution.py:68
  26.9 12.7 %collective-permute-start.6 = (bf16[160,1024]{1,0:T(8,128)(2,1)S(1)}, bf16[160,1024]{1,0:T(8,128)(2,1)S(1)}, u32[]{:S(2)}, u32[]{:S(2)}) collective-permute-start(bf16[160,1024]{1,0:T(8,128)(2,1)S(1)} %get-tuple-element.44), channel_id=1, source_target_pairs={{4,0},{8,4},{12,8},{16,12},{20,16},{24,20},{28,24},{5,1},{9,5},{13... | collective-permute-start | bytes 983048 | tf_op jit(solution)/shard_map/ppermute | solution.py:74
  28.5 17.9 %collective-permute-start.8 = (bf16[64,4096]{1,0:T(8,128)(2,1)S(1)}, bf16[64,4096]{1,0:T(8,128)(2,1)S(1)}, u32[]{:S(2)}, u32[]{:S(2)}) collective-permute-start(bf16[64,4096]{1,0:T(8,128)(2,1)S(1)} %slice.39.refs_2_), channel_id=1, source_target_pairs={{0,2},{1,3},{2,0},{3,1},{4,6},{5,7},{6,4},{7,5},{8,10},{9,11},{10,... | collective-permute-start | bytes 1572872 | tf_op jit(solution)/shard_map/ppermute | solution.py:68
  32.1 10.4 %collective-permute-start.5 = (f32[64,64]{1,0:T(8,128)S(1)}, f32[64,64]{1,0:T(8,128)S(1)}, u32[]{:S(2)}, u32[]{:S(2)}) collective-permute-start(f32[64,64]{1,0:T(8,128)S(1)} %slice.32), channel_id=1, source_target_pairs={{0,16},{4,20},{8,24},{12,28},{16,0},{20,4},{24,8},{28,12},{1,17},{... | collective-permute-start | bytes 49160 | tf_op jit(solution)/shard_map/ppermute | solution.py:68
  42.6 3.8 %collective-permute-start.7 = (f32[32,64]{1,0:T(8,128)S(1)}, f32[32,64]{1,0:T(8,128)S(1)}, u32[]{:S(2)}, u32[]{:S(2)}) collective-permute-start(f32[32,64]{1,0:T(8,128)S(1)} %slice.33), channel_id=1, source_target_pairs={{0,8},{4,12},{8,0},{12,4},{16,24},{20,28},{24,16},{28,20},{1,9},{5... | collective-permute-start | bytes 24584 | tf_op jit(solution)/shard_map/ppermute | solution.py:68
  46.4 4.1 %collective-permute-start.9 = (f32[16,64]{1,0:T(8,128)S(1)}, f32[16,64]{1,0:T(8,128)S(1)}, u32[]{:S(2)}, u32[]{:S(2)}) collective-permute-start(f32[16,64]{1,0:T(8,128)S(1)} %slice.35), channel_id=1, source_target_pairs={{0,4},{4,0},{8,12},{12,8},{16,20},{20,16},{24,28},{28,24},{1,5},{5... | collective-permute-start | bytes 12296 | tf_op jit(solution)/shard_map/ppermute | solution.py:68
where the time goes:
time: 51.7 us; the launch traced here: 51.4 us
  Pallas kernels  24.6 us (48%)
  starting transfers between devices  15.7 us (30%)
  waiting for transfers between devices  9.91 us (19%)
  between operations  0.83 us (2%)
    pallas_call x10, Pallas kernels, called(): pl.pallas_call(kernel, name=name, in_specs=[pl.BlockSpec(memory_space=spa...  24.6 us
    ppermute x8, starting transfers between devices, exchanged(): lax.ppermute(value, axis, [(index, index ^ bit) for index in range(count)])  10.9 us
    ppermute x8, waiting for transfers between devices, exchanged(): lax.ppermute(value, axis, [(index, index ^ bit) for index in range(count)])  6.41 us
    ppermute x2, starting transfers between devices, passed_along(): lax.ppermute(value, axis, [(source, source + steps) for source in range(i...  4.74 us
    ppermute x2, waiting for transfers between devices, passed_along(): lax.ppermute(value, axis, [(source, source + steps) for source in range(i...  3.5 us
  transfers between devices with their start and end apart: 10, of which 5 were waited for; matrix products, arithmetic and copies ran while one was open for 1% of the time, Pallas kernels for 37%

commit v1 on v0

--- a/solution.py
+++ b/solution.py
@@ -327,7 +327,7 @@
         if kept < rows:
             term_refs[1][:, cols] = terms[kept:]
 
-    repeated(w_ref.shape[1] // chunk, project)
+    unrolled(w_ref.shape[1] // chunk, project)
 
 
 def project(mixer_out, out_weight, after, n_tp):
@@ -616,18 +616,20 @@
     apart = share % EDGE == 0
     lags = lag_sums(lgrad, gext, group_count, n_ctx if apart else 1, after)
     fgs = feature_grads(lgrad, later, qgrad, feats, firsts, skip, bwd_table)
-    proj_grad = short_grads(fgs, weights)
-    arrived = lags
+    arrived, proj_grad = lags, None
     for position, bit in enumerate(reversed(bits_of(n_ctx)) if apart else ()):
         if position:
             lags = lags[: bit * share * 2] + arrived
         arrived = exchanged(lags[bit * share :], "ctx", bit)
         if position == 0:
-            arrived, later = lax.optimization_barrier((arrived, later))
+            arrived, fgs = lax.optimization_barrier((arrived, fgs))
         if position == 1:
-            arrived, final = lax.optimization_barrier((arrived, final))
+            proj_grad = short_grads(fgs, weights)
+            arrived, final, proj_grad = lax.optimization_barrier((arrived, final, proj_grad))
     if not apart:
         lags = arrived = lax.psum_scatter(lags, "ctx", scatter_dimension=0, tiled=True)
+    if proj_grad is None:
+        proj_grad = short_grads(fgs, weights)
     factor = 1.0 / math.sqrt(rows * n_ctx * (channels // group_count))
     if not apart:
         arrived = final

time: 51.7 us -> 50.4 us (0.975)
  waiting for transfers between devices: 9.91 us -> 7.69 us
  starting transfers between devices: 15.7 us -> 17.6 us
  Pallas kernels: 24.6 us -> 23.4 us
    ppermute x8, waiting for transfers between devices: 6.41 us -> 4.36 us  [exchanged(): lax.ppermute(value, axis, [(index, index ^ bit) for index in range(count)])]
    ppermute x8, starting transfers between devices: 10.9 us -> 12.7 us  [exchanged(): lax.ppermute(value, axis, [(index, index ^ bit) for index in range(count)])]
    pallas_call x10, Pallas kernels: 24.6 us -> 23.4 us  [called(): pl.pallas_call(kernel, name=name, in_specs=[pl.BlockSpec(memory_space=spa...]
  transfers between devices with their start and end apart: 10 -> 10, of which waited for: 5 -> 5; matrix products, arithmetic and copies ran while one was open for 1% -> 1% of each run, Pallas kernels for 37% -> 38%
where the time goes in v1:
time: 50.4 us; the launch traced here: 50.1 us
  Pallas kernels  23.4 us (46%)
  starting transfers between devices  17.6 us (35%)
  waiting for transfers between devices  7.69 us (15%)
  between operations  0.99 us (2%)
    pallas_call x10, Pallas kernels, called(): pl.pallas_call(kernel, name=name, in_specs=[pl.BlockSpec(memory_space=spa...  23.4 us
    ppermute x8, starting transfers between devices, exchanged(): lax.ppermute(value, axis, [(index, index ^ bit) for index in range(count)])  12.7 us
    ppermute x2, starting transfers between devices, passed_along(): lax.ppermute(value, axis, [(source, source + steps) for source in range(i...  4.92 us
    ppermute x8, waiting for transfers between devices, exchanged(): lax.ppermute(value, axis, [(index, index ^ bit) for index in range(count)])  4.36 us
    ppermute x2, waiting for transfers between devices, passed_along(): lax.ppermute(value, axis, [(source, source + steps) for source in range(i...  3.32 us
  transfers between devices with their start and end apart: 10, of which 5 were waited for; matrix products, arithmetic and copies ran while one was open for 1% of the time, Pallas kernels for 38%

profile of v1, /device:TPU:0, one launch (start us, length us, event | category | flops | bytes accessed | tf_op | source)
XLA Modules:
  0.0 50.1 jit_solution(17174159098666900477)
XLA Ops:
  0.6 3.0 %collective-permute-start.2 = (bf16[64,4096]{1,0:T(8,128)(2,1)}, bf16[64,4096]{1,0:T(8,128)(2,1)S(1)}, u32[]{:S(2)}, u32[]{:S(2)}) collective-permute-start(bf16[64,4096]{1,0:T(8,128)(2,1)} %refs_0_.1), channel_id=1, source_target_pairs={{0,2},{1,3},{2,0},{3,1},{4,6},{5,7},{6,4},{7,5},{8,10},{9,11},{10,... | collective-permute-start | bytes 1572872 | tf_op jit(solution)/shard_map/ppermute | solution.py:68
  3.6 0.0 collective-permute-start.1
  3.6 1.9 %gated_tail.1.after_hbm = bf16[160,1024]{1,0:T(8,128)(2,1)S(1)} custom-call(bf16[3,256,1024]{2,1,0:T(8,128)(2,1)} %proj_hbm.3, f32[3,7,1024]{2,1,0:T(8,128)} %sw_hbm.3), custom_call_target="tpu_custom_call" | custom-call | flops 1 | bytes 1 | tf_op jit(solution)/shard_map/gated_tail/pallas_call | solution.py:29
  5.5 3.4 %collective-permute-start = (bf16[160,1024]{1,0:T(8,128)(2,1)S(1)}, bf16[160,1024]{1,0:T(8,128)(2,1)S(1)}, u32[]{:S(2)}, u32[]{:S(2)}) collective-permute-start(bf16[160,1024]{1,0:T(8,128)(2,1)S(1)} %gated_tail.1.after_hbm), channel_id=1, source_target_pairs={{0,4},{4,8},{8,12},{12,16},{16,20},{20,24},{24,28},{1,5},{5,9},{9,... | collective-permute-start | bytes 983048 | tf_op jit(solution)/shard_map/ppermute | solution.py:74
  8.9 5.6 %prepare.1 = (f32[3,256,1024]{2,1,0:T(8,128)S(1)}, f32[3,8,1024]{2,1,0:T(8,128)S(1)}, bf16[256,1024]{1,0:T(8,128)(2,1)S(1)}, bf16[8192,256]{1,0:T(8,128)(2,1)S(1...) custom-call(bf16[3,256,1024]{2,1,0:T(8,128)(2,1)} %proj_hbm.3, ...), custom_call_target="tpu_custom_call" | custom-call | flops 99999997952 | bytes 1 | tf_op jit(solution)/shard_map/prepare/pallas_call | solution.py:29
  14.6 1.2 %collective-permute-done.2.refs_2_ = bf16[64,4096]{1,0:T(8,128)(2,1)S(1)} collective-permute-done((bf16[64,4096]{1,0:T(8,128)(2,1)}, bf16[64,4096]{1,0:T(8,128)(2,1)S(1)}, u32[]{:S(2)}, u32[]{:S(2)}) %collective-permute-start.2) | collective-permute-done | bytes 524320 | tf_op jit(solution)/shard_map/ppermute | solution.py:68
  15.8 0.0 collective-permute-start.3
  15.8 0.8 %collective-permute-done.halo_ref = bf16[160,1024]{1,0:T(8,128)(2,1)S(1)} collective-permute-done((bf16[160,1024]{1,0:T(8,128)(2,1)S(1)}, bf16[160,1024]{1,0:T(8,128)(2,1)S(1)}, u32[]{:S(2)}, u32[]{:S(2)}) %collective-permute-start) | collective-permute-done | bytes 327712 | tf_op jit(solution)/shard_map/ppermute | solution.py:74
  16.6 1.5 %forward.1 = (f32[3,8,1024]{2,1,0:T(8,128)S(1)}, f32[256,1024]{1,0:T(8,128)S(1)}, bf16[384,1024]{1,0:T(8,128)(2,1)S(1)}, bf16[256,1024]{1,0:T(8,128)(2,1)S(1)}) custom-call(f32[3,256,1024]{2,1,0:T(8,128)S(1)} %get-tuple-element.29.feat_ref, f32[3,8,1024]{2,1,0:T(8,128)S(1)} %get-tuple-element.30.edge_ref, bf16[256,1024]{1,0:T(8,128)(2,1)S(1)} %get-tuple-element.31.gated_ref, ...), custom_call_target="tpu_custom_call" | custom-call | flops 99999997952 | bytes 1 | tf_op jit(solution)/shard_map/forward/pallas_call | solution.py:29
  18.1 0.0 collective-permute-done.1.refs_2_.refs_1_
  18.1 0.0 collective-permute-done.3.refs_3_
  18.1 0.0 copy-start
  18.1 3.5 %project.1 = (bf16[128,4096]{1,0:T(8,128)(2,1)S(1)}, bf16[128,4096]{1,0:T(8,128)(2,1)S(1)}) custom-call(bf16[256,1024]{1,0:T(8,128)(2,1)S(1)} %get-tuple-element.35.refs_0_, bf16[1024,4096]{1,0:T(8,128)(2,1)S(1)} %get-tuple-element.36.refs_1_.refs_4_, bf16[64,4096]{1,0:T(8,128)(2,1)} %collective-permute-done.1.refs_2_.refs_1_, ...), custom_call_target="tpu_custom_call" | custom-call | flops 1 | bytes 1 | tf_op jit(solution)/shard_map/project/pallas_call | solution.py:29
  21.6 0.1 collective-permute-start.4
  21.7 0.0 copy-done
  21.7 3.5 %grads.1.grad_ref = f32[256,1024]{1,0:T(8,128)S(1)} custom-call(bf16[64,4096]{1,0:T(8,128)(2,1)S(1)} %copy-done, bf16[64,4096]{1,0:T(8,128)(2,1)} %collective-permute-done.1.refs_2_.refs_1_, bf16[64,4096]{1,0:T(8,128)(2,1)S(1)} %collective-permute-done.2.refs_2_, bf16[64,4096]{1,0:T(8,128)(2,1)S(1)} %collective-permute-done.3.refs_3_, ...), custom_call_target="tpu_custom_call" | custom-call | flops 1 | bytes 1 | tf_op jit(solution)/shard_map/grads/pallas_call | solution.py:29
  25.2 0.5 backward.1
  25.7 1.5 %collective-permute-start.6 = (bf16[160,1024]{1,0:T(8,128)(2,1)S(1)}, bf16[160,1024]{1,0:T(8,128)(2,1)S(1)}, u32[]{:S(2)}, u32[]{:S(2)}) collective-permute-start(bf16[160,1024]{1,0:T(8,128)(2,1)S(1)} %get-tuple-element.46), channel_id=1, source_target_pairs={{4,0},{8,4},{12,8},{16,12},{20,16},{24,20},{28,24},{5,1},{9,5},{13... | collective-permute-start | bytes 983048 | tf_op jit(solution)/shard_map/ppermute | solution.py:74
  27.1 0.0 collective-permute-done.4
  27.1 0.3 convert_add_fusion
  27.4 0.1 slice.39.refs_2_
  27.5 1.5 %collective-permute-start.8 = (bf16[64,4096]{1,0:T(8,128)(2,1)S(1)}, bf16[64,4096]{1,0:T(8,128)(2,1)S(1)}, u32[]{:S(2)}, u32[]{:S(2)}) collective-permute-start(bf16[64,4096]{1,0:T(8,128)(2,1)S(1)} %slice.39.refs_2_), channel_id=1, source_target_pairs={{0,2},{1,3},{2,0},{3,1},{4,6},{5,7},{6,4},{7,5},{8,10},{9,11},{10,... | collective-permute-start | bytes 1572872 | tf_op jit(solution)/shard_map/ppermute | solution.py:68
  29.0 2.1 %lag_sums.1 = f32[128,64]{1,0:T(8,128)S(1)} custom-call(bf16[256,1024]{1,0:T(8,128)(2,1)S(1)} %get-tuple-element.44.refs_0_.lgrad_ref, bf16[384,1024]{1,0:T(8,128)(2,1)S(1)} %get-tuple-element.45.refs_1_, bf16[64,4096]{1,0:T(8,128)(2,1)S(1)} %slice.39.refs_2_), custom_call_target="tpu_custom_call" | custom-call | flops 1 | bytes 1 | tf_op jit(solution)/shard_map/lag_sums/pallas_call | solution.py:29
  31.1 4.7 %collective-permute-start.5 = (f32[64,64]{1,0:T(8,128)S(1)}, f32[64,64]{1,0:T(8,128)S(1)}, u32[]{:S(2)}, u32[]{:S(2)}) collective-permute-start(f32[64,64]{1,0:T(8,128)S(1)} %slice.32), channel_id=1, source_target_pairs={{0,16},{4,20},{8,24},{12,28},{16,0},{20,4},{24,8},{28,12},{1,17},{... | collective-permute-start | bytes 49160 | tf_op jit(solution)/shard_map/ppermute | solution.py:68
  35.9 2.5 %collective-permute-done.6.head_ref = bf16[160,1024]{1,0:T(8,128)(2,1)S(1)} collective-permute-done((bf16[160,1024]{1,0:T(8,128)(2,1)S(1)}, bf16[160,1024]{1,0:T(8,128)(2,1)S(1)}, u32[]{:S(2)}, u32[]{:S(2)}) %collective-permute-start.6) | collective-permute-done | bytes 327712 | tf_op jit(solution)/shard_map/ppermute | solution.py:74
  38.4 1.6 %feature_grads.1.fg_ref = f32[8,3,264,128]{3,2,1,0:T(8,128)S(1)} custom-call(bf16[256,1024]{1,0:T(8,128)(2,1)S(1)} %get-tuple-element.44.refs_0_.lgrad_ref, bf16[160,1024]{1,0:T(8,128)(2,1)S(1)} %collective-permute-done.6.head_ref, f32[256,1024]{1,0:T(8,128)S(1)} %get-tuple-element.47.qgrad_ref, f32[3,256,1024]{2,1,0:T(8,128)S(1)} %get-tuple-element.29.feat_ref, ...), custom_call_target="tpu_custom_call" | custom-call | flops 1 | bytes 1 | tf_op jit(solution)/shard_map/feature_grads/pallas_call | solution.py:29
  40.0 1.4 %collective-permute-done.5 = f32[64,64]{1,0:T(8,128)S(1)} collective-permute-done((f32[64,64]{1,0:T(8,128)S(1)}, f32[64,64]{1,0:T(8,128)S(1)}, u32[]{:S(2)}, u32[]{:S(2)}) %collective-permute-start.5) | collective-permute-done | bytes 16416 | tf_op jit(solution)/shard_map/ppermute | solution.py:68
  41.4 1.5 %collective-permute-start.7 = (f32[32,64]{1,0:T(8,128)S(1)}, f32[32,64]{1,0:T(8,128)S(1)}, u32[]{:S(2)}, u32[]{:S(2)}) collective-permute-start(f32[32,64]{1,0:T(8,128)S(1)} %slice.33), channel_id=1, source_target_pairs={{0,8},{4,12},{8,0},{12,4},{16,24},{20,28},{24,16},{28,20},{1,9},{5... | collective-permute-start | bytes 24584 | tf_op jit(solution)/shard_map/ppermute | solution.py:68
  42.9 2.3 %short_grads.1 = f32[3,256,1024]{2,1,0:T(8,128)} custom-call(f32[8,3,264,128]{3,2,1,0:T(8,128)S(1)} %feature_grads.1.fg_ref, f32[3,7,1024]{2,1,0:T(8,128)S(1)} %get-tuple-element.32.sw_ref), custom_call_target="tpu_custom_call" | custom-call | flops 1 | bytes 1 | tf_op jit(solution)/shard_map/short_grads/pallas_call | solution.py:29
  45.3 0.0 collective-permute-done.7
  45.3 0.0 collective-permute-done.8.refs_1_
  45.3 1.8 %collective-permute-start.9 = (f32[16,64]{1,0:T(8,128)S(1)}, f32[16,64]{1,0:T(8,128)S(1)}, u32[]{:S(2)}, u32[]{:S(2)}) collective-permute-start(f32[16,64]{1,0:T(8,128)S(1)} %slice.35), channel_id=1, source_target_pairs={{0,4},{4,0},{8,12},{12,8},{16,20},{20,16},{24,28},{28,24},{1,5},{5... | collective-permute-start | bytes 12296 | tf_op jit(solution)/shard_map/ppermute | solution.py:68
  47.1 0.1 slice.29.refs_0_
  47.2 1.8 %collective-permute-done.9.refs_3_ = f32[16,64]{1,0:T(8,128)S(1)} collective-permute-done((f32[16,64]{1,0:T(8,128)S(1)}, f32[16,64]{1,0:T(8,128)S(1)}, u32[]{:S(2)}, u32[]{:S(2)}) %collective-permute-start.9) | collective-permute-done | bytes 4128 | tf_op jit(solution)/shard_map/ppermute | solution.py:68
  49.0 0.9 %last.1 = (bf16[64,4096]{1,0:T(8,128)(2,1)}, f32[16,64]{1,0:T(8,128)}) custom-call(f32[64,4096]{1,0:T(8,128)S(1)} %slice.29.refs_0_, bf16[64,4096]{1,0:T(8,128)(2,1)S(1)} %collective-permute-done.8.refs_1_, f32[32,64]{1,0:T(8,128)S(1)} %slice_add_fusion.1.refs_2_, f32[16,64]{1,0:T(8,128)S(1)} %collective-permute-done.9.refs_3_), custom_call_target="tpu_custom_call" | custom-call | flops 1 | bytes 1 | tf_op jit(solution)/shard_map/last/pallas_call | solution.py:29
  (5 shorter events, 0.0 us)
Async XLA Ops:
  0.6 15.1 %collective-permute-start.2 = (bf16[64,4096]{1,0:T(8,128)(2,1)}, bf16[64,4096]{1,0:T(8,128)(2,1)S(1)}, u32[]{:S(2)}, u32[]{:S(2)}) collective-permute-start(bf16[64,4096]{1,0:T(8,128)(2,1)} %refs_0_.1), channel_id=1, source_target_pairs={{0,2},{1,3},{2,0},{3,1},{4,6},{5,7},{6,4},{7,5},{8,10},{9,11},{10,... | collective-permute-start | bytes 1572872 | tf_op jit(solution)/shard_map/ppermute | solution.py:68
  3.6 14.5 %collective-permute-start.1 = (bf16[64,4096]{1,0:T(8,128)(2,1)}, bf16[64,4096]{1,0:T(8,128)(2,1)}, u32[]{:S(2)}, u32[]{:S(2)}) collective-permute-start(bf16[64,4096]{1,0:T(8,128)(2,1)} %refs_0_.1), channel_id=1, source_target_pairs={{0,1},{1,0},{2,3},{3,2},{4,5},{5,4},{6,7},{7,6},{8,9},{9,8},{10,11... | collective-permute-start | bytes 1572872 | tf_op jit(solution)/shard_map/ppermute | solution.py:68
  5.5 11.1 %collective-permute-start = (bf16[160,1024]{1,0:T(8,128)(2,1)S(1)}, bf16[160,1024]{1,0:T(8,128)(2,1)S(1)}, u32[]{:S(2)}, u32[]{:S(2)}) collective-permute-start(bf16[160,1024]{1,0:T(8,128)(2,1)S(1)} %gated_tail.1.after_hbm), channel_id=1, source_target_pairs={{0,4},{4,8},{8,12},{12,16},{16,20},{20,24},{24,28},{1,5},{5,9},{9,... | collective-permute-start | bytes 983048 | tf_op jit(solution)/shard_map/ppermute | solution.py:74
  15.8 2.3 %collective-permute-start.3 = (bf16[64,4096]{1,0:T(8,128)(2,1)S(1)}, bf16[64,4096]{1,0:T(8,128)(2,1)S(1)}, u32[]{:S(2)}, u32[]{:S(2)}) collective-permute-start(bf16[64,4096]{1,0:T(8,128)(2,1)S(1)} %collective-permute-done.2.refs_2_), channel_id=1, source_target_pairs={{0,1},{1,0},{2,3},{3,2},{4,5},{5,4},{6,7},{7,6},{8,9},{9,8},{10,11... | collective-permute-start | bytes 1572872 | tf_op jit(solution)/shard_map/ppermute | solution.py:68
  18.1 3.6 %copy-start = (bf16[64,4096]{1,0:T(8,128)(2,1)S(1)}, bf16[64,4096]{1,0:T(8,128)(2,1)}, u32[]{:S(2)}) copy-start(bf16[64,4096]{1,0:T(8,128)(2,1)} %refs_0_.1) | copy-start | bytes 1572868
  21.6 5.5 %collective-permute-start.4 = (bf16[128,4096]{1,0:T(8,128)(2,1)S(1)}, bf16[128,4096]{1,0:T(8,128)(2,1)S(1)}, u32[]{:S(2)}, u32[]{:S(2)}) collective-permute-start(bf16[128,4096]{1,0:T(8,128)(2,1)S(1)} %get-tuple-element.38), channel_id=1, source_target_pairs={{0,1},{1,0},{2,3},{3,2},{4,5},{5,4},{6,7},{7,6},{8,9},{9,8},{10,11... | collective-permute-start | bytes 3145736 | tf_op jit(solution)/shard_map/ppermute | solution.py:68
  25.7 12.7 %collective-permute-start.6 = (bf16[160,1024]{1,0:T(8,128)(2,1)S(1)}, bf16[160,1024]{1,0:T(8,128)(2,1)S(1)}, u32[]{:S(2)}, u32[]{:S(2)}) collective-permute-start(bf16[160,1024]{1,0:T(8,128)(2,1)S(1)} %get-tuple-element.46), channel_id=1, source_target_pairs={{4,0},{8,4},{12,8},{16,12},{20,16},{24,20},{28,24},{5,1},{9,5},{13... | collective-permute-start | bytes 983048 | tf_op jit(solution)/shard_map/ppermute | solution.py:74
  27.5 17.8 %collective-permute-start.8 = (bf16[64,4096]{1,0:T(8,128)(2,1)S(1)}, bf16[64,4096]{1,0:T(8,128)(2,1)S(1)}, u32[]{:S(2)}, u32[]{:S(2)}) collective-permute-start(bf16[64,4096]{1,0:T(8,128)(2,1)S(1)} %slice.39.refs_2_), channel_id=1, source_target_pairs={{0,2},{1,3},{2,0},{3,1},{4,6},{5,7},{6,4},{7,5},{8,10},{9,11},{10,... | collective-permute-start | bytes 1572872 | tf_op jit(solution)/shard_map/ppermute | solution.py:68
  31.1 10.2 %collective-permute-start.5 = (f32[64,64]{1,0:T(8,128)S(1)}, f32[64,64]{1,0:T(8,128)S(1)}, u32[]{:S(2)}, u32[]{:S(2)}) collective-permute-start(f32[64,64]{1,0:T(8,128)S(1)} %slice.32), channel_id=1, source_target_pairs={{0,16},{4,20},{8,24},{12,28},{16,0},{20,4},{24,8},{28,12},{1,17},{... | collective-permute-start | bytes 49160 | tf_op jit(solution)/shard_map/ppermute | solution.py:68
  41.4 3.9 %collective-permute-start.7 = (f32[32,64]{1,0:T(8,128)S(1)}, f32[32,64]{1,0:T(8,128)S(1)}, u32[]{:S(2)}, u32[]{:S(2)}) collective-permute-start(f32[32,64]{1,0:T(8,128)S(1)} %slice.33), channel_id=1, source_target_pairs={{0,8},{4,12},{8,0},{12,4},{16,24},{20,28},{24,16},{28,20},{1,9},{5... | collective-permute-start | bytes 24584 | tf_op jit(solution)/shard_map/ppermute | solution.py:68
  45.3 3.7 %collective-permute-start.9 = (f32[16,64]{1,0:T(8,128)S(1)}, f32[16,64]{1,0:T(8,128)S(1)}, u32[]{:S(2)}, u32[]{:S(2)}) collective-permute-start(f32[16,64]{1,0:T(8,128)S(1)} %slice.35), channel_id=1, source_target_pairs={{0,4},{4,0},{8,12},{12,8},{16,20},{20,16},{24,28},{28,24},{1,5},{5... | collective-permute-start | bytes 12296 | tf_op jit(solution)/shard_map/ppermute | solution.py:68

commit v2 on v1

--- a/solution.py
+++ b/solution.py
@@ -318,7 +318,7 @@
     order = halving_order(rows // own)
     ordered = jnp.concatenate([mix_ref[rows_of(me ^ k, own), :] for k in order], axis=0)
     kept = term_refs[0].shape[0]
-    chunk = 512
+    chunk = 2048
 
     def project(block):
         cols = pl.ds(multiple(block * chunk, chunk), chunk)

time: 50.4 us -> 50.4 us (level)
  no operation moved by 1% of the time
where the time goes in v2:
time: 50.4 us; the launch traced here: 50.1 us
  Pallas kernels  23.4 us (46%)
  starting transfers between devices  17.6 us (35%)
  waiting for transfers between devices  7.69 us (15%)
  between operations  0.99 us (2%)
    pallas_call x10, Pallas kernels, called(): pl.pallas_call(kernel, name=name, in_specs=[pl.BlockSpec(memory_space=spa...  23.4 us
    ppermute x8, starting transfers between devices, exchanged(): lax.ppermute(value, axis, [(index, index ^ bit) for index in range(count)])  12.7 us
    ppermute x2, starting transfers between devices, passed_along(): lax.ppermute(value, axis, [(source, source + steps) for source in range(i...  4.92 us
    ppermute x8, waiting for transfers between devices, exchanged(): lax.ppermute(value, axis, [(index, index ^ bit) for index in range(count)])  4.36 us
    ppermute x2, waiting for transfers between devices, passed_along(): lax.ppermute(value, axis, [(source, source + steps) for source in range(i...  3.32 us
  transfers between devices with their start and end apart: 10, of which 5 were waited for; matrix products, arithmetic and copies ran while one was open for 1% of the time, Pallas kernels for 38%

profile of v2, /device:TPU:0, one launch (start us, length us, event | category | flops | bytes accessed | tf_op | source)
XLA Modules:
  0.0 50.1 jit_solution(17174159098666900477)
XLA Ops:
  0.6 3.0 %collective-permute-start.2 = (bf16[64,4096]{1,0:T(8,128)(2,1)}, bf16[64,4096]{1,0:T(8,128)(2,1)S(1)}, u32[]{:S(2)}, u32[]{:S(2)}) collective-permute-start(bf16[64,4096]{1,0:T(8,128)(2,1)} %refs_0_.1), channel_id=1, source_target_pairs={{0,2},{1,3},{2,0},{3,1},{4,6},{5,7},{6,4},{7,5},{8,10},{9,11},{10,... | collective-permute-start | bytes 1572872 | tf_op jit(solution)/shard_map/ppermute | solution.py:68
  3.6 0.0 collective-permute-start.1
  3.6 1.9 %gated_tail.1.after_hbm = bf16[160,1024]{1,0:T(8,128)(2,1)S(1)} custom-call(bf16[3,256,1024]{2,1,0:T(8,128)(2,1)} %proj_hbm.3, f32[3,7,1024]{2,1,0:T(8,128)} %sw_hbm.3), custom_call_target="tpu_custom_call" | custom-call | flops 1 | bytes 1 | tf_op jit(solution)/shard_map/gated_tail/pallas_call | solution.py:29
  5.5 3.4 %collective-permute-start = (bf16[160,1024]{1,0:T(8,128)(2,1)S(1)}, bf16[160,1024]{1,0:T(8,128)(2,1)S(1)}, u32[]{:S(2)}, u32[]{:S(2)}) collective-permute-start(bf16[160,1024]{1,0:T(8,128)(2,1)S(1)} %gated_tail.1.after_hbm), channel_id=1, source_target_pairs={{0,4},{4,8},{8,12},{12,16},{16,20},{20,24},{24,28},{1,5},{5,9},{9,... | collective-permute-start | bytes 983048 | tf_op jit(solution)/shard_map/ppermute | solution.py:74
  8.9 5.6 %prepare.1 = (f32[3,256,1024]{2,1,0:T(8,128)S(1)}, f32[3,8,1024]{2,1,0:T(8,128)S(1)}, bf16[256,1024]{1,0:T(8,128)(2,1)S(1)}, bf16[8192,256]{1,0:T(8,128)(2,1)S(1...) custom-call(bf16[3,256,1024]{2,1,0:T(8,128)(2,1)} %proj_hbm.3, ...), custom_call_target="tpu_custom_call" | custom-call | flops 99999997952 | bytes 1 | tf_op jit(solution)/shard_map/prepare/pallas_call | solution.py:29
  14.6 1.2 %collective-permute-done.2.refs_2_ = bf16[64,4096]{1,0:T(8,128)(2,1)S(1)} collective-permute-done((bf16[64,4096]{1,0:T(8,128)(2,1)}, bf16[64,4096]{1,0:T(8,128)(2,1)S(1)}, u32[]{:S(2)}, u32[]{:S(2)}) %collective-permute-start.2) | collective-permute-done | bytes 524320 | tf_op jit(solution)/shard_map/ppermute | solution.py:68
  15.8 0.0 collective-permute-start.3
  15.8 0.8 %collective-permute-done.halo_ref = bf16[160,1024]{1,0:T(8,128)(2,1)S(1)} collective-permute-done((bf16[160,1024]{1,0:T(8,128)(2,1)S(1)}, bf16[160,1024]{1,0:T(8,128)(2,1)S(1)}, u32[]{:S(2)}, u32[]{:S(2)}) %collective-permute-start) | collective-permute-done | bytes 327712 | tf_op jit(solution)/shard_map/ppermute | solution.py:74
  16.6 1.5 %forward.1 = (f32[3,8,1024]{2,1,0:T(8,128)S(1)}, f32[256,1024]{1,0:T(8,128)S(1)}, bf16[384,1024]{1,0:T(8,128)(2,1)S(1)}, bf16[256,1024]{1,0:T(8,128)(2,1)S(1)}) custom-call(f32[3,256,1024]{2,1,0:T(8,128)S(1)} %get-tuple-element.29.feat_ref, f32[3,8,1024]{2,1,0:T(8,128)S(1)} %get-tuple-element.30.edge_ref, bf16[256,1024]{1,0:T(8,128)(2,1)S(1)} %get-tuple-element.31.gated_ref, ...), custom_call_target="tpu_custom_call" | custom-call | flops 99999997952 | bytes 1 | tf_op jit(solution)/shard_map/forward/pallas_call | solution.py:29
  18.1 0.0 collective-permute-done.1.refs_2_.refs_1_
  18.1 0.0 collective-permute-done.3.refs_3_
  18.1 0.0 copy-start
  18.1 3.5 %project.1 = (bf16[128,4096]{1,0:T(8,128)(2,1)S(1)}, bf16[128,4096]{1,0:T(8,128)(2,1)S(1)}) custom-call(bf16[256,1024]{1,0:T(8,128)(2,1)S(1)} %get-tuple-element.35.refs_0_, bf16[1024,4096]{1,0:T(8,128)(2,1)S(1)} %get-tuple-element.36.refs_1_.refs_4_, bf16[64,4096]{1,0:T(8,128)(2,1)} %collective-permute-done.1.refs_2_.refs_1_, ...), custom_call_target="tpu_custom_call" | custom-call | flops 1 | bytes 1 | tf_op jit(solution)/shard_map/project/pallas_call | solution.py:29
  21.6 0.1 collective-permute-start.4
  21.7 0.0 copy-done
  21.7 3.5 %grads.1.grad_ref = f32[256,1024]{1,0:T(8,128)S(1)} custom-call(bf16[64,4096]{1,0:T(8,128)(2,1)S(1)} %copy-done, bf16[64,4096]{1,0:T(8,128)(2,1)} %collective-permute-done.1.refs_2_.refs_1_, bf16[64,4096]{1,0:T(8,128)(2,1)S(1)} %collective-permute-done.2.refs_2_, bf16[64,4096]{1,0:T(8,128)(2,1)S(1)} %collective-permute-done.3.refs_3_, ...), custom_call_target="tpu_custom_call" | custom-call | flops 1 | bytes 1 | tf_op jit(solution)/shard_map/grads/pallas_call | solution.py:29
  25.2 0.5 backward.1
  25.7 1.5 %collective-permute-start.6 = (bf16[160,1024]{1,0:T(8,128)(2,1)S(1)}, bf16[160,1024]{1,0:T(8,128)(2,1)S(1)}, u32[]{:S(2)}, u32[]{:S(2)}) collective-permute-start(bf16[160,1024]{1,0:T(8,128)(2,1)S(1)} %get-tuple-element.46), channel_id=1, source_target_pairs={{4,0},{8,4},{12,8},{16,12},{20,16},{24,20},{28,24},{5,1},{9,5},{13... | collective-permute-start | bytes 983048 | tf_op jit(solution)/shard_map/ppermute | solution.py:74
  27.1 0.0 collective-permute-done.4
  27.1 0.3 convert_add_fusion
  27.4 0.1 slice.39.refs_2_
  27.5 1.5 %collective-permute-start.8 = (bf16[64,4096]{1,0:T(8,128)(2,1)S(1)}, bf16[64,4096]{1,0:T(8,128)(2,1)S(1)}, u32[]{:S(2)}, u32[]{:S(2)}) collective-permute-start(bf16[64,4096]{1,0:T(8,128)(2,1)S(1)} %slice.39.refs_2_), channel_id=1, source_target_pairs={{0,2},{1,3},{2,0},{3,1},{4,6},{5,7},{6,4},{7,5},{8,10},{9,11},{10,... | collective-permute-start | bytes 1572872 | tf_op jit(solution)/shard_map/ppermute | solution.py:68
  29.0 2.1 %lag_sums.1 = f32[128,64]{1,0:T(8,128)S(1)} custom-call(bf16[256,1024]{1,0:T(8,128)(2,1)S(1)} %get-tuple-element.44.refs_0_.lgrad_ref, bf16[384,1024]{1,0:T(8,128)(2,1)S(1)} %get-tuple-element.45.refs_1_, bf16[64,4096]{1,0:T(8,128)(2,1)S(1)} %slice.39.refs_2_), custom_call_target="tpu_custom_call" | custom-call | flops 1 | bytes 1 | tf_op jit(solution)/shard_map/lag_sums/pallas_call | solution.py:29
  31.1 4.7 %collective-permute-start.5 = (f32[64,64]{1,0:T(8,128)S(1)}, f32[64,64]{1,0:T(8,128)S(1)}, u32[]{:S(2)}, u32[]{:S(2)}) collective-permute-start(f32[64,64]{1,0:T(8,128)S(1)} %slice.32), channel_id=1, source_target_pairs={{0,16},{4,20},{8,24},{12,28},{16,0},{20,4},{24,8},{28,12},{1,17},{... | collective-permute-start | bytes 49160 | tf_op jit(solution)/shard_map/ppermute | solution.py:68
  35.9 2.5 %collective-permute-done.6.head_ref = bf16[160,1024]{1,0:T(8,128)(2,1)S(1)} collective-permute-done((bf16[160,1024]{1,0:T(8,128)(2,1)S(1)}, bf16[160,1024]{1,0:T(8,128)(2,1)S(1)}, u32[]{:S(2)}, u32[]{:S(2)}) %collective-permute-start.6) | collective-permute-done | bytes 327712 | tf_op jit(solution)/shard_map/ppermute | solution.py:74
  38.4 1.6 %feature_grads.1.fg_ref = f32[8,3,264,128]{3,2,1,0:T(8,128)S(1)} custom-call(bf16[256,1024]{1,0:T(8,128)(2,1)S(1)} %get-tuple-element.44.refs_0_.lgrad_ref, bf16[160,1024]{1,0:T(8,128)(2,1)S(1)} %collective-permute-done.6.head_ref, f32[256,1024]{1,0:T(8,128)S(1)} %get-tuple-element.47.qgrad_ref, f32[3,256,1024]{2,1,0:T(8,128)S(1)} %get-tuple-element.29.feat_ref, ...), custom_call_target="tpu_custom_call" | custom-call | flops 1 | bytes 1 | tf_op jit(solution)/shard_map/feature_grads/pallas_call | solution.py:29
  40.0 1.4 %collective-permute-done.5 = f32[64,64]{1,0:T(8,128)S(1)} collective-permute-done((f32[64,64]{1,0:T(8,128)S(1)}, f32[64,64]{1,0:T(8,128)S(1)}, u32[]{:S(2)}, u32[]{:S(2)}) %collective-permute-start.5) | collective-permute-done | bytes 16416 | tf_op jit(solution)/shard_map/ppermute | solution.py:68
  41.4 1.5 %collective-permute-start.7 = (f32[32,64]{1,0:T(8,128)S(1)}, f32[32,64]{1,0:T(8,128)S(1)}, u32[]{:S(2)}, u32[]{:S(2)}) collective-permute-start(f32[32,64]{1,0:T(8,128)S(1)} %slice.33), channel_id=1, source_target_pairs={{0,8},{4,12},{8,0},{12,4},{16,24},{20,28},{24,16},{28,20},{1,9},{5... | collective-permute-start | bytes 24584 | tf_op jit(solution)/shard_map/ppermute | solution.py:68
  42.9 2.3 %short_grads.1 = f32[3,256,1024]{2,1,0:T(8,128)} custom-call(f32[8,3,264,128]{3,2,1,0:T(8,128)S(1)} %feature_grads.1.fg_ref, f32[3,7,1024]{2,1,0:T(8,128)S(1)} %get-tuple-element.32.sw_ref), custom_call_target="tpu_custom_call" | custom-call | flops 1 | bytes 1 | tf_op jit(solution)/shard_map/short_grads/pallas_call | solution.py:29
  45.3 0.0 collective-permute-done.7
  45.3 0.0 collective-permute-done.8.refs_1_
  45.3 1.8 %collective-permute-start.9 = (f32[16,64]{1,0:T(8,128)S(1)}, f32[16,64]{1,0:T(8,128)S(1)}, u32[]{:S(2)}, u32[]{:S(2)}) collective-permute-start(f32[16,64]{1,0:T(8,128)S(1)} %slice.35), channel_id=1, source_target_pairs={{0,4},{4,0},{8,12},{12,8},{16,20},{20,16},{24,28},{28,24},{1,5},{5... | collective-permute-start | bytes 12296 | tf_op jit(solution)/shard_map/ppermute | solution.py:68
  47.1 0.1 slice.29.refs_0_
  47.2 1.8 %collective-permute-done.9.refs_3_ = f32[16,64]{1,0:T(8,128)S(1)} collective-permute-done((f32[16,64]{1,0:T(8,128)S(1)}, f32[16,64]{1,0:T(8,128)S(1)}, u32[]{:S(2)}, u32[]{:S(2)}) %collective-permute-start.9) | collective-permute-done | bytes 4128 | tf_op jit(solution)/shard_map/ppermute | solution.py:68
  49.0 0.9 %last.1 = (bf16[64,4096]{1,0:T(8,128)(2,1)}, f32[16,64]{1,0:T(8,128)}) custom-call(f32[64,4096]{1,0:T(8,128)S(1)} %slice.29.refs_0_, bf16[64,4096]{1,0:T(8,128)(2,1)S(1)} %collective-permute-done.8.refs_1_, f32[32,64]{1,0:T(8,128)S(1)} %slice_add_fusion.1.refs_2_, f32[16,64]{1,0:T(8,128)S(1)} %collective-permute-done.9.refs_3_), custom_call_target="tpu_custom_call" | custom-call | flops 1 | bytes 1 | tf_op jit(solution)/shard_map/last/pallas_call | solution.py:29
  (5 shorter events, 0.0 us)
Async XLA Ops:
  0.6 15.1 %collective-permute-start.2 = (bf16[64,4096]{1,0:T(8,128)(2,1)}, bf16[64,4096]{1,0:T(8,128)(2,1)S(1)}, u32[]{:S(2)}, u32[]{:S(2)}) collective-permute-start(bf16[64,4096]{1,0:T(8,128)(2,1)} %refs_0_.1), channel_id=1, source_target_pairs={{0,2},{1,3},{2,0},{3,1},{4,6},{5,7},{6,4},{7,5},{8,10},{9,11},{10,... | collective-permute-start | bytes 1572872 | tf_op jit(solution)/shard_map/ppermute | solution.py:68
  3.6 14.5 %collective-permute-start.1 = (bf16[64,4096]{1,0:T(8,128)(2,1)}, bf16[64,4096]{1,0:T(8,128)(2,1)}, u32[]{:S(2)}, u32[]{:S(2)}) collective-permute-start(bf16[64,4096]{1,0:T(8,128)(2,1)} %refs_0_.1), channel_id=1, source_target_pairs={{0,1},{1,0},{2,3},{3,2},{4,5},{5,4},{6,7},{7,6},{8,9},{9,8},{10,11... | collective-permute-start | bytes 1572872 | tf_op jit(solution)/shard_map/ppermute | solution.py:68
  5.5 11.1 %collective-permute-start = (bf16[160,1024]{1,0:T(8,128)(2,1)S(1)}, bf16[160,1024]{1,0:T(8,128)(2,1)S(1)}, u32[]{:S(2)}, u32[]{:S(2)}) collective-permute-start(bf16[160,1024]{1,0:T(8,128)(2,1)S(1)} %gated_tail.1.after_hbm), channel_id=1, source_target_pairs={{0,4},{4,8},{8,12},{12,16},{16,20},{20,24},{24,28},{1,5},{5,9},{9,... | collective-permute-start | bytes 983048 | tf_op jit(solution)/shard_map/ppermute | solution.py:74
  15.8 2.3 %collective-permute-start.3 = (bf16[64,4096]{1,0:T(8,128)(2,1)S(1)}, bf16[64,4096]{1,0:T(8,128)(2,1)S(1)}, u32[]{:S(2)}, u32[]{:S(2)}) collective-permute-start(bf16[64,4096]{1,0:T(8,128)(2,1)S(1)} %collective-permute-done.2.refs_2_), channel_id=1, source_target_pairs={{0,1},{1,0},{2,3},{3,2},{4,5},{5,4},{6,7},{7,6},{8,9},{9,8},{10,11... | collective-permute-start | bytes 1572872 | tf_op jit(solution)/shard_map/ppermute | solution.py:68
  18.1 3.6 %copy-start = (bf16[64,4096]{1,0:T(8,128)(2,1)S(1)}, bf16[64,4096]{1,0:T(8,128)(2,1)}, u32[]{:S(2)}) copy-start(bf16[64,4096]{1,0:T(8,128)(2,1)} %refs_0_.1) | copy-start | bytes 1572868
  21.6 5.5 %collective-permute-start.4 = (bf16[128,4096]{1,0:T(8,128)(2,1)S(1)}, bf16[128,4096]{1,0:T(8,128)(2,1)S(1)}, u32[]{:S(2)}, u32[]{:S(2)}) collective-permute-start(bf16[128,4096]{1,0:T(8,128)(2,1)S(1)} %get-tuple-element.38), channel_id=1, source_target_pairs={{0,1},{1,0},{2,3},{3,2},{4,5},{5,4},{6,7},{7,6},{8,9},{9,8},{10,11... | collective-permute-start | bytes 3145736 | tf_op jit(solution)/shard_map/ppermute | solution.py:68
  25.7 12.7 %collective-permute-start.6 = (bf16[160,1024]{1,0:T(8,128)(2,1)S(1)}, bf16[160,1024]{1,0:T(8,128)(2,1)S(1)}, u32[]{:S(2)}, u32[]{:S(2)}) collective-permute-start(bf16[160,1024]{1,0:T(8,128)(2,1)S(1)} %get-tuple-element.46), channel_id=1, source_target_pairs={{4,0},{8,4},{12,8},{16,12},{20,16},{24,20},{28,24},{5,1},{9,5},{13... | collective-permute-start | bytes 983048 | tf_op jit(solution)/shard_map/ppermute | solution.py:74
  27.5 17.8 %collective-permute-start.8 = (bf16[64,4096]{1,0:T(8,128)(2,1)S(1)}, bf16[64,4096]{1,0:T(8,128)(2,1)S(1)}, u32[]{:S(2)}, u32[]{:S(2)}) collective-permute-start(bf16[64,4096]{1,0:T(8,128)(2,1)S(1)} %slice.39.refs_2_), channel_id=1, source_target_pairs={{0,2},{1,3},{2,0},{3,1},{4,6},{5,7},{6,4},{7,5},{8,10},{9,11},{10,... | collective-permute-start | bytes 1572872 | tf_op jit(solution)/shard_map/ppermute | solution.py:68
  31.1 10.2 %collective-permute-start.5 = (f32[64,64]{1,0:T(8,128)S(1)}, f32[64,64]{1,0:T(8,128)S(1)}, u32[]{:S(2)}, u32[]{:S(2)}) collective-permute-start(f32[64,64]{1,0:T(8,128)S(1)} %slice.32), channel_id=1, source_target_pairs={{0,16},{4,20},{8,24},{12,28},{16,0},{20,4},{24,8},{28,12},{1,17},{... | collective-permute-start | bytes 49160 | tf_op jit(solution)/shard_map/ppermute | solution.py:68
  41.4 3.9 %collective-permute-start.7 = (f32[32,64]{1,0:T(8,128)S(1)}, f32[32,64]{1,0:T(8,128)S(1)}, u32[]{:S(2)}, u32[]{:S(2)}) collective-permute-start(f32[32,64]{1,0:T(8,128)S(1)} %slice.33), channel_id=1, source_target_pairs={{0,8},{4,12},{8,0},{12,4},{16,24},{20,28},{24,16},{28,20},{1,9},{5... | collective-permute-start | bytes 24584 | tf_op jit(solution)/shard_map/ppermute | solution.py:68
  45.3 3.7 %collective-permute-start.9 = (f32[16,64]{1,0:T(8,128)S(1)}, f32[16,64]{1,0:T(8,128)S(1)}, u32[]{:S(2)}, u32[]{:S(2)}) collective-permute-start(f32[16,64]{1,0:T(8,128)S(1)} %slice.35), channel_id=1, source_target_pairs={{0,4},{4,0},{8,12},{12,8},{16,20},{20,16},{24,28},{28,24},{1,5},{5... | collective-permute-start | bytes 12296 | tf_op jit(solution)/shard_map/ppermute | solution.py:68
